TPU v7x, 32 devices: a whole 2x2x4 slice. The times are simulated.
32 devices in a mesh: gx: 4 (over y, x), gy: 8 (over z, core).
Axes of the slice: x: 2, y: 2, z: 4, core: 2. Of those that a mesh axis runs over, the one named last changes fastest.
Arguments:
- element_fields: bfloat16 [16384, 5, 512], P(('gx', 'gy')), may hold values from -6 to 6
- ref_coords: float32 [3, 65536], P(None, ('gx', 'gy')), may hold values from -1 to 1
- local_element: int32 [65536], P(('gx', 'gy')), may hold values from 0 to 511
- owner: int32 [65536, 1], P(('gx', 'gy')), may hold values from 0 to 31; in each aligned block of 2048 rows (0 to 2047, 2048 to 4095, ...) at most 256 rows name the same one
- point_angle: float32 [65536], P(('gx', 'gy')), may hold values from -3.140625 to 3.140625
- point_axial: float32 [65536], P(('gx', 'gy')), may hold values from 0 to 8
- panel_weight: float32 [65536], P(('gx', 'gy')), may hold values from 0.5 to 2
- obs_radius: float32 [256], replicated, may hold values from 3 to 30
- obs_angle: float32 [256], replicated, may hold values from -3.140625 to 3.140625
- obs_axial: float32 [256], replicated, may hold values from -8 to 16
- step_phase: float32 [32], replicated, may hold values from -3.140625 to 3.140625
- observer_slot: int32 [256], replicated, may hold values from 0 to 255, each once
- prior_spectra: float32 [2, 32, 256], P(None, None, ('gx', 'gy')), may hold values from -6 to 6
Outputs:
- surface_values: float32 [5, 65536], P(None, ('gx', 'gy'))
- spectra: float32 [2, 32, 256], P(None, None, ('gx', 'gy'))
Inputs may be any that keep to these rules, and one draw needn't show every extreme that they name: Among the points of one device at most 256 have the same owner, and in every draw some device has exactly 256 points owned by one device. `observer_slot`: each output column is named by exactly one observer.
All inputs are finite; a program needn't handle non-finite values.
Results may differ from a plain program's by a relative error of at most 0.0003.
Values sent between devices are 32-bit elements; how exact they have to be, the bound alone decides.
A program may use at most 64 MiB of HBM per device.

v0:
```python
import math

import jax
import jax.numpy as jnp
import numpy as np
from jax import lax
from jax.sharding import PartitionSpec as P

NODES = 512
FIELDS = 5


gll_nodes = np.array(
    [
        -1.0,
        -0.8717401485096066,
        -0.5917001814331423,
        -0.2092992179024789,
        0.2092992179024789,
        0.5917001814331423,
        0.8717401485096066,
        1.0,
    ]
)
omega_base = 0.25


def lagrange(coord):
    columns = []
    for first in range(8):
        product = jnp.ones_like(coord)
        divisor = 1.0
        for second in range(8):
            if second != first:
                product = product * (coord - float(gll_nodes[second]))
                divisor = divisor * (gll_nodes[first] - gll_nodes[second])
        columns.append(product * float(1.0 / divisor))
    return jnp.stack(columns)


def node_weights(coords):
    along_r = lagrange(coords[0])
    along_s = lagrange(coords[1])
    along_t = lagrange(coords[2])
    pair_rs = along_r[:, None, :] * along_s[None, :, :]
    return (pair_rs[:, :, None, :] * along_t[None, None, :, :]).reshape(NODES, coords.shape[1])


def interpolate(fields, elem_ids, coords):
    slot_count = elem_ids.shape[0]
    block_rows = math.gcd(slot_count, 1024)
    block_count = slot_count // block_rows

    def sample(pieces):
        weights = node_weights(pieces[1])
        gathered = jnp.take(fields, pieces[0], axis=0).astype(jnp.float32)
        return jnp.einsum("nfq,qn->fn", gathered, weights)

    sampled = lax.map(
        sample,
        (
            elem_ids.reshape(block_count, block_rows),
            coords.reshape(3, block_count, block_rows).transpose(1, 0, 2),
        ),
    )
    return sampled.transpose(1, 0, 2).reshape(FIELDS, slot_count)


def spectra_terms(
    values, angle, axial, weight, obs_radius, obs_angle, obs_axial, step_phase, norm_scale
):
    cos_p = jnp.cos(angle)
    sin_p = jnp.sin(angle)
    step_x = (obs_radius * jnp.cos(obs_angle))[None, :] - cos_p[:, None]
    step_y = (obs_radius * jnp.sin(obs_angle))[None, :] - sin_p[:, None]
    step_z = obs_axial[None, :] - axial[:, None]
    distance = jnp.sqrt(step_x * step_x + step_y * step_y + step_z * step_z)
    density = values[0]
    vel_x = values[1]
    vel_y = values[2]
    vel_z = values[3]
    pressure = values[4]
    mass_flux = density * (vel_x * cos_p + vel_y * sin_p)
    radial = (step_x * cos_p[:, None] + step_y * sin_p[:, None]) / distance
    radial_vel = (
        vel_x[:, None] * step_x + vel_y[:, None] * step_y + vel_z[:, None] * step_z
    ) / distance
    amplitude = (
        weight[:, None]
        * (mass_flux[:, None] + pressure[:, None] * radial + mass_flux[:, None] * radial_vel)
        * obs_radius[None, :]
        / distance
        * norm_scale
    )
    harmonic = omega_base * jnp.arange(1, step_phase.shape[0] + 1, dtype=jnp.float32)
    phases = distance[:, :, None] * harmonic[None, None, :] + step_phase[None, None, :]
    cos_sum = jnp.sum(amplitude[:, :, None] * jnp.cos(phases), axis=0).T
    sin_sum = -jnp.sum(amplitude[:, :, None] * jnp.sin(phases), axis=0).T
    return jnp.stack([cos_sum, sin_sum])


def on_device(
    element_fields,
    ref_coords,
    local_element,
    owner,
    point_angle,
    point_axial,
    panel_weight,
    obs_radius,
    obs_angle,
    obs_axial,
    step_phase,
    observer_slot,
    prior_spectra,
):
    devices = lax.axis_size(("gx", "gy"))
    points = local_element.shape[0]
    capacity = 4 * points // devices
    target = owner[:, 0]
    rank_rows = math.gcd(points, 512)
    rank_blocks = points // rank_rows
    one_hot = (
        (target[:, None] == jnp.arange(devices, dtype=jnp.int32)[None, :])
        .astype(jnp.bfloat16)
        .reshape(rank_blocks, rank_rows, devices)
    )
    strict_lower = (jnp.arange(rank_rows)[:, None] > jnp.arange(rank_rows)[None, :]).astype(
        jnp.bfloat16
    )
    within = jnp.einsum("ij,bjd->bid", strict_lower, one_hot, preferred_element_type=jnp.float32)
    hot_float = one_hot.astype(jnp.float32)
    totals = jnp.sum(hot_float, axis=1)
    offsets = jnp.cumsum(totals, axis=0) - totals
    slot_rank = (
        jnp.sum(hot_float * (within + offsets[:, None, :]), axis=2)
        .reshape(points)
        .astype(jnp.int32)
    )
    position = target * capacity + slot_rank
    send_ids = jnp.zeros((devices * capacity,), jnp.int32).at[position].set(local_element)
    send_coords = jnp.zeros((3, devices * capacity), jnp.float32).at[:, position].set(ref_coords)
    elem_ids = lax.all_to_all(
        send_ids.reshape(1, devices, capacity),
        ("gx", "gy"),
        split_axis=1,
        concat_axis=1,
        tiled=True,
    )
    coords = lax.all_to_all(
        send_coords.reshape(3, devices, capacity),
        ("gx", "gy"),
        split_axis=1,
        concat_axis=1,
        tiled=True,
    )
    slot_count = elem_ids.shape[1] * elem_ids.shape[2]
    interpolated = interpolate(
        element_fields, elem_ids.reshape(slot_count), coords.reshape(3, slot_count)
    )
    served = interpolated.reshape(FIELDS, elem_ids.shape[1], elem_ids.shape[2])
    replies = lax.all_to_all(served, ("gx", "gy"), split_axis=1, concat_axis=1, tiled=True)
    surface_values = replies.reshape(FIELDS, devices * capacity)[:, position]
    norm_scale = 1.0 / math.sqrt(points * devices)
    green_rows = math.gcd(points, 256)
    green_blocks = points // green_rows

    def accumulate(running, pieces):
        return (
            running
            + spectra_terms(
                pieces[0],
                pieces[1],
                pieces[2],
                pieces[3],
                obs_radius,
                obs_angle,
                obs_axial,
                step_phase,
                norm_scale,
            ),
            None,
        )

    starting = jnp.zeros((2, step_phase.shape[0], obs_radius.shape[0]), jnp.float32)
    summed, unused = lax.scan(
        accumulate,
        starting,
        (
            surface_values.reshape(FIELDS, green_blocks, green_rows).transpose(1, 0, 2),
            point_angle.reshape(green_blocks, green_rows),
            point_axial.reshape(green_blocks, green_rows),
            panel_weight.reshape(green_blocks, green_rows),
        ),
    )
    placed = jnp.zeros_like(summed).at[:, :, observer_slot].set(summed)
    owned_part = lax.psum_scatter(placed, ("gx", "gy"), scatter_dimension=2, tiled=True)
    return (surface_values, prior_spectra + owned_part)


def solution(mesh):
    return jax.shard_map(
        on_device,
        mesh=mesh,
        in_specs=(
            P(("gx", "gy"), None, None),
            P(None, ("gx", "gy")),
            P(("gx", "gy")),
            P(("gx", "gy"), None),
            P(("gx", "gy")),
            P(("gx", "gy")),
            P(("gx", "gy")),
            P(),
            P(),
            P(),
            P(),
            P(),
            P(None, None, ("gx", "gy")),
        ),
        out_specs=(P(None, ("gx", "gy")), P(None, None, ("gx", "gy"))),
        check_vma=False,
    )
```

profile of v0, /device:TPU:0, one launch (start us, length us, event | category | flops | bytes accessed | tf_op | source)
XLA Modules:
  0.0 727.4 jit_solution(15651725334842922083)
XLA Ops:
  10.6 8.8 %scatter_custom_fusion.1 = s32[8192]{0:T(1024)} fusion(s32[2048]{0:T(1024)S(1)} %bitcast.631, s32[2048]{0:T(1024)} %param.19, s32[]{:T(128)} %constant.202.clone.1), kind=kCustom, calls=%fused_computation.212 | custom fusion | bytes 33280 | tf_op jit(solution)/shard_map/scatter | solution.py:141
  28.8 8.1 %scatter_custom_fusion = f32[3,8192]{0,1:T(8,128)} fusion(s32[2048]{0:T(1024)S(1)} %bitcast.632, f32[2048,3]{1,0:T(8,128)} %copy.45, f32[]{:T(128)} %constant.203.clone.1), kind=kCustom, calls=%fused_computation.199 | custom fusion | bytes 98816 | tf_op jit(solution)/shard_map/scatter | solution.py:142
  50.0 8.0 %all-to-all-done = f32[3,32,256]{2,0,1:T(4,128)S(1)} async-done(((f32[3,32,256]{2,0,1:T(4,128)}), f32[3,32,256]{2,0,1:T(4,128)S(1)}, u32[]{:S(2)}, u32[]{:S(2)}) %all-to-all-start) | async-done | bytes 98336 | tf_op jit(solution)/shard_map/all_to_all | solution.py:150
  58.1 251.4 %while.26 = (s32[]{:T(128)}, f32[8,5,1024]{2,1,0:T(8,128)}, f32[8,3,1024]{2,0,1:T(8,128)S(1)}, s32[8,1024]{1,0:T(8,128)S(1)}, bf16[512,5,512]{2,1,0:T(8,128)(2,1)}, /*index=5*/s32[]{:T(128)}, s32[]{:T(128)}, s32[]{}, s32[]{}) while((s32[]{:T(128)}, f32[8,5,1024]{2,1,0:T(8,128)}, f32[8,3,1024]{2,0,1:T(8,128)S(1)}, s32[8,1024]{1,0:T(8,128)S(1)}, ...), condition=%wide.region_6.7_spmd, body=%wide.region_5.6_spmd.sunk | while | flops 11257860 | bytes 33618608 | solution.py:59
  60.8 12.0 %gather_fusion = bf16[1024,5,512]{2,1,0:T(8,128)(2,1)} fusion(bf16[512,5,512]{2,1,0:T(8,128)(2,1)} %get-tuple-element.604, s32[1024]{0:T(1024)S(1)} %broadcast_clamp_fusion.3), kind=kCustom, calls=%fused_computation.clone.1 | custom fusion | bytes 10489856 | tf_op jit(solution)/shard_map/while/body/eval_jaxpr/jit(_take)/gather | solution.py:56
  72.8 15.9 %multiply_reduce_fusion.5 = f32[1024,5]{1,0:T(8,128)S(1)} fusion(f32[1024,512]{1,0:T(8,128)S(1)} %copy-done, bf16[1024,5,512]{2,1,0:T(8,128)(2,1)} %gather_fusion, pred[1024]{0:T(1024)(128)(4,1)S(1)} %compare_and_fusion.2), kind=kLoop, calls=%fused_computation.46.clone.1 | loop fusion | flops 10480640 | bytes 7361536 | tf_op jit(solution)/shard_map/while
  92.2 12.0 %gather_fusion = bf16[1024,5,512]{2,1,0:T(8,128)(2,1)} fusion(bf16[512,5,512]{2,1,0:T(8,128)(2,1)} %get-tuple-element.604, s32[1024]{0:T(1024)S(1)} %broadcast_clamp_fusion.3), kind=kCustom, calls=%fused_computation.clone.1 | custom fusion | bytes 10489856 | tf_op jit(solution)/shard_map/while/body/eval_jaxpr/jit(_take)/gather | solution.py:56
  104.3 15.9 %multiply_reduce_fusion.5 = f32[1024,5]{1,0:T(8,128)S(1)} fusion(f32[1024,512]{1,0:T(8,128)S(1)} %copy-done, bf16[1024,5,512]{2,1,0:T(8,128)(2,1)} %gather_fusion, pred[1024]{0:T(1024)(128)(4,1)S(1)} %compare_and_fusion.2), kind=kLoop, calls=%fused_computation.46.clone.1 | loop fusion | flops 10480640 | bytes 7361536 | tf_op jit(solution)/shard_map/while
  123.7 12.0 %gather_fusion = bf16[1024,5,512]{2,1,0:T(8,128)(2,1)} fusion(bf16[512,5,512]{2,1,0:T(8,128)(2,1)} %get-tuple-element.604, s32[1024]{0:T(1024)S(1)} %broadcast_clamp_fusion.3), kind=kCustom, calls=%fused_computation.clone.1 | custom fusion | bytes 10489856 | tf_op jit(solution)/shard_map/while/body/eval_jaxpr/jit(_take)/gather | solution.py:56
  135.7 15.9 %multiply_reduce_fusion.5 = f32[1024,5]{1,0:T(8,128)S(1)} fusion(f32[1024,512]{1,0:T(8,128)S(1)} %copy-done, bf16[1024,5,512]{2,1,0:T(8,128)(2,1)} %gather_fusion, pred[1024]{0:T(1024)(128)(4,1)S(1)} %compare_and_fusion.2), kind=kLoop, calls=%fused_computation.46.clone.1 | loop fusion | flops 10480640 | bytes 7361536 | tf_op jit(solution)/shard_map/while
  155.1 12.0 %gather_fusion = bf16[1024,5,512]{2,1,0:T(8,128)(2,1)} fusion(bf16[512,5,512]{2,1,0:T(8,128)(2,1)} %get-tuple-element.604, s32[1024]{0:T(1024)S(1)} %broadcast_clamp_fusion.3), kind=kCustom, calls=%fused_computation.clone.1 | custom fusion | bytes 10489856 | tf_op jit(solution)/shard_map/while/body/eval_jaxpr/jit(_take)/gather | solution.py:56
  167.1 15.9 %multiply_reduce_fusion.5 = f32[1024,5]{1,0:T(8,128)S(1)} fusion(f32[1024,512]{1,0:T(8,128)S(1)} %copy-done, bf16[1024,5,512]{2,1,0:T(8,128)(2,1)} %gather_fusion, pred[1024]{0:T(1024)(128)(4,1)S(1)} %compare_and_fusion.2), kind=kLoop, calls=%fused_computation.46.clone.1 | loop fusion | flops 10480640 | bytes 7361536 | tf_op jit(solution)/shard_map/while
  186.5 12.0 %gather_fusion = bf16[1024,5,512]{2,1,0:T(8,128)(2,1)} fusion(bf16[512,5,512]{2,1,0:T(8,128)(2,1)} %get-tuple-element.604, s32[1024]{0:T(1024)S(1)} %broadcast_clamp_fusion.3), kind=kCustom, calls=%fused_computation.clone.1 | custom fusion | bytes 10489856 | tf_op jit(solution)/shard_map/while/body/eval_jaxpr/jit(_take)/gather | solution.py:56
  198.5 15.9 %multiply_reduce_fusion.5 = f32[1024,5]{1,0:T(8,128)S(1)} fusion(f32[1024,512]{1,0:T(8,128)S(1)} %copy-done, bf16[1024,5,512]{2,1,0:T(8,128)(2,1)} %gather_fusion, pred[1024]{0:T(1024)(128)(4,1)S(1)} %compare_and_fusion.2), kind=kLoop, calls=%fused_computation.46.clone.1 | loop fusion | flops 10480640 | bytes 7361536 | tf_op jit(solution)/shard_map/while
  217.9 12.0 %gather_fusion = bf16[1024,5,512]{2,1,0:T(8,128)(2,1)} fusion(bf16[512,5,512]{2,1,0:T(8,128)(2,1)} %get-tuple-element.604, s32[1024]{0:T(1024)S(1)} %broadcast_clamp_fusion.3), kind=kCustom, calls=%fused_computation.clone.1 | custom fusion | bytes 10489856 | tf_op jit(solution)/shard_map/while/body/eval_jaxpr/jit(_take)/gather | solution.py:56
  230.0 15.9 %multiply_reduce_fusion.5 = f32[1024,5]{1,0:T(8,128)S(1)} fusion(f32[1024,512]{1,0:T(8,128)S(1)} %copy-done, bf16[1024,5,512]{2,1,0:T(8,128)(2,1)} %gather_fusion, pred[1024]{0:T(1024)(128)(4,1)S(1)} %compare_and_fusion.2), kind=kLoop, calls=%fused_computation.46.clone.1 | loop fusion | flops 10480640 | bytes 7361536 | tf_op jit(solution)/shard_map/while
  249.3 12.0 %gather_fusion = bf16[1024,5,512]{2,1,0:T(8,128)(2,1)} fusion(bf16[512,5,512]{2,1,0:T(8,128)(2,1)} %get-tuple-element.604, s32[1024]{0:T(1024)S(1)} %broadcast_clamp_fusion.3), kind=kCustom, calls=%fused_computation.clone.1 | custom fusion | bytes 10489856 | tf_op jit(solution)/shard_map/while/body/eval_jaxpr/jit(_take)/gather | solution.py:56
  261.4 15.9 %multiply_reduce_fusion.5 = f32[1024,5]{1,0:T(8,128)S(1)} fusion(f32[1024,512]{1,0:T(8,128)S(1)} %copy-done, bf16[1024,5,512]{2,1,0:T(8,128)(2,1)} %gather_fusion, pred[1024]{0:T(1024)(128)(4,1)S(1)} %compare_and_fusion.2), kind=kLoop, calls=%fused_computation.46.clone.1 | loop fusion | flops 10480640 | bytes 7361536 | tf_op jit(solution)/shard_map/while
  280.8 12.0 %gather_fusion = bf16[1024,5,512]{2,1,0:T(8,128)(2,1)} fusion(bf16[512,5,512]{2,1,0:T(8,128)(2,1)} %get-tuple-element.604, s32[1024]{0:T(1024)S(1)} %broadcast_clamp_fusion.3), kind=kCustom, calls=%fused_computation.clone.1 | custom fusion | bytes 10489856 | tf_op jit(solution)/shard_map/while/body/eval_jaxpr/jit(_take)/gather | solution.py:56
  292.8 15.9 %multiply_reduce_fusion.5 = f32[1024,5]{1,0:T(8,128)S(1)} fusion(f32[1024,512]{1,0:T(8,128)S(1)} %copy-done, bf16[1024,5,512]{2,1,0:T(8,128)(2,1)} %gather_fusion, pred[1024]{0:T(1024)(128)(4,1)S(1)} %compare_and_fusion.2), kind=kLoop, calls=%fused_computation.46.clone.1 | loop fusion | flops 10480640 | bytes 7361536 | tf_op jit(solution)/shard_map/while
  312.5 9.7 %all-to-all-done.2 = f32[5,32,256]{2,0,1:T(8,128)S(1)} async-done(((f32[5,32,256]{2,0,1:T(8,128)}), f32[5,32,256]{2,0,1:T(8,128)S(1)}, u32[]{:S(2)}, u32[]{:S(2)}) %all-to-all-start.2) | async-done | bytes 163872 | tf_op jit(solution)/shard_map/all_to_all | solution.py:162
  324.8 7.6 %gather_fusion.1 = f32[2048,5]{1,0:T(8,128)S(1)} fusion(f32[5,8192]{0,1:T(8,128)} %bitcast.604, s32[2048]{0:T(1024)S(1)} %broadcast_clamp_fusion.1), kind=kCustom, calls=%fused_computation.1 | custom fusion | bytes 90112 | tf_op jit(solution)/shard_map/gather | solution.py:163
  332.8 253.6 %while.27 = (s32[]{:T(128)}, f32[2,32,256]{2,1,0:T(8,128)S(1)}, f32[8,256]{1,0:T(8,128)S(1)}, f32[8,5,256]{2,1,0:T(8,128)S(1)}, f32[8,256]{1,0:T(8,128)S(1)}, /*...) while((s32[]{:T(128)}, f32[2,32,256]{2,1,0:T(8,128)S(1)}, ...), condition=%wide.region_10.11_spmd.clone, body=%wide.region_7.10_spmd.clone.sunk | while | flops 14328903 | bytes 1413747 | solution.py:186
  333.3 31.1 %multiply_reduce_fusion.6 = (f32[256,32]{0,1:T(8,128)S(1)}, f32[256,32]{0,1:T(8,128)S(1)}) fusion(f32[32]{0:T(128)S(1)} %get-tuple-element.653, f32[32]{0:T(128)S(1)} %add_multiply_fusion.4, f32[256,256]{1,0:T(8,128)S(1)} %get-tuple-element.578, f32[256,256]{1,0:T(8,128)S(1)} %get-tuple-element.579), kind=kLoop, calls=%fused_computation.6.clone.1 | loop fusion | flops 12566528 | bytes 590080 | tf_op jit(solution)/shard_map/while/body/eval_jaxpr/reduce_sum | solution.py:97
  365.0 31.1 %multiply_reduce_fusion.6 = (f32[256,32]{0,1:T(8,128)S(1)}, f32[256,32]{0,1:T(8,128)S(1)}) fusion(f32[32]{0:T(128)S(1)} %get-tuple-element.653, f32[32]{0:T(128)S(1)} %add_multiply_fusion.4, f32[256,256]{1,0:T(8,128)S(1)} %get-tuple-element.578, f32[256,256]{1,0:T(8,128)S(1)} %get-tuple-element.579), kind=kLoop, calls=%fused_computation.6.clone.1 | loop fusion | flops 12566528 | bytes 590080 | tf_op jit(solution)/shard_map/while/body/eval_jaxpr/reduce_sum | solution.py:97
  396.7 31.1 %multiply_reduce_fusion.6 = (f32[256,32]{0,1:T(8,128)S(1)}, f32[256,32]{0,1:T(8,128)S(1)}) fusion(f32[32]{0:T(128)S(1)} %get-tuple-element.653, f32[32]{0:T(128)S(1)} %add_multiply_fusion.4, f32[256,256]{1,0:T(8,128)S(1)} %get-tuple-element.578, f32[256,256]{1,0:T(8,128)S(1)} %get-tuple-element.579), kind=kLoop, calls=%fused_computation.6.clone.1 | loop fusion | flops 12566528 | bytes 590080 | tf_op jit(solution)/shard_map/while/body/eval_jaxpr/reduce_sum | solution.py:97
  428.4 31.1 %multiply_reduce_fusion.6 = (f32[256,32]{0,1:T(8,128)S(1)}, f32[256,32]{0,1:T(8,128)S(1)}) fusion(f32[32]{0:T(128)S(1)} %get-tuple-element.653, f32[32]{0:T(128)S(1)} %add_multiply_fusion.4, f32[256,256]{1,0:T(8,128)S(1)} %get-tuple-element.578, f32[256,256]{1,0:T(8,128)S(1)} %get-tuple-element.579), kind=kLoop, calls=%fused_computation.6.clone.1 | loop fusion | flops 12566528 | bytes 590080 | tf_op jit(solution)/shard_map/while/body/eval_jaxpr/reduce_sum | solution.py:97
  460.1 31.1 %multiply_reduce_fusion.6 = (f32[256,32]{0,1:T(8,128)S(1)}, f32[256,32]{0,1:T(8,128)S(1)}) fusion(f32[32]{0:T(128)S(1)} %get-tuple-element.653, f32[32]{0:T(128)S(1)} %add_multiply_fusion.4, f32[256,256]{1,0:T(8,128)S(1)} %get-tuple-element.578, f32[256,256]{1,0:T(8,128)S(1)} %get-tuple-element.579), kind=kLoop, calls=%fused_computation.6.clone.1 | loop fusion | flops 12566528 | bytes 590080 | tf_op jit(solution)/shard_map/while/body/eval_jaxpr/reduce_sum | solution.py:97
  491.8 31.1 %multiply_reduce_fusion.6 = (f32[256,32]{0,1:T(8,128)S(1)}, f32[256,32]{0,1:T(8,128)S(1)}) fusion(f32[32]{0:T(128)S(1)} %get-tuple-element.653, f32[32]{0:T(128)S(1)} %add_multiply_fusion.4, f32[256,256]{1,0:T(8,128)S(1)} %get-tuple-element.578, f32[256,256]{1,0:T(8,128)S(1)} %get-tuple-element.579), kind=kLoop, calls=%fused_computation.6.clone.1 | loop fusion | flops 12566528 | bytes 590080 | tf_op jit(solution)/shard_map/while/body/eval_jaxpr/reduce_sum | solution.py:97
  523.5 31.1 %multiply_reduce_fusion.6 = (f32[256,32]{0,1:T(8,128)S(1)}, f32[256,32]{0,1:T(8,128)S(1)}) fusion(f32[32]{0:T(128)S(1)} %get-tuple-element.653, f32[32]{0:T(128)S(1)} %add_multiply_fusion.4, f32[256,256]{1,0:T(8,128)S(1)} %get-tuple-element.578, f32[256,256]{1,0:T(8,128)S(1)} %get-tuple-element.579), kind=kLoop, calls=%fused_computation.6.clone.1 | loop fusion | flops 12566528 | bytes 590080 | tf_op jit(solution)/shard_map/while/body/eval_jaxpr/reduce_sum | solution.py:97
  555.2 31.1 %multiply_reduce_fusion.6 = (f32[256,32]{0,1:T(8,128)S(1)}, f32[256,32]{0,1:T(8,128)S(1)}) fusion(f32[32]{0:T(128)S(1)} %get-tuple-element.653, f32[32]{0:T(128)S(1)} %add_multiply_fusion.4, f32[256,256]{1,0:T(8,128)S(1)} %get-tuple-element.578, f32[256,256]{1,0:T(8,128)S(1)} %get-tuple-element.579), kind=kLoop, calls=%fused_computation.6.clone.1 | loop fusion | flops 12566528 | bytes 590080 | tf_op jit(solution)/shard_map/while/body/eval_jaxpr/reduce_sum | solution.py:97
  595.2 124.0 %all-reduce.3.cloned.1.call-done = f32[2,32,256]{1,0,2:T(2,128)} async-done(((f32[2,32,256]{1,0,2:T(2,128)}), f32[2,32,256]{1,0,2:T(2,128)}) %all-reduce.3.cloned.1.call-update) | async-done | bytes 65552
  (253 shorter events, 73.3 us)
Async XLA Ops:
  7.2 33.2 %copy-start.1 = (bf16[512,5,512]{2,0,1:T(8,128)(2,1)S(1)}, bf16[512,5,512]{2,0,1:T(8,128)(2,1)}, u32[]{:S(2)}) copy-start(bf16[512,5,512]{2,0,1:T(8,128)(2,1)} %param.17) | copy-start | bytes 7864324
  10.6 39.3 %copy-start.3 = (f32[256]{0:T(256)S(1)}, f32[256]{0:T(256)}, u32[]{:S(2)}) copy-start(f32[256]{0:T(256)} %param.24) | copy-start | bytes 3076
  10.6 39.3 %copy-start.10 = (f32[256]{0:T(256)S(1)}, f32[256]{0:T(256)}, u32[]{:S(2)}) copy-start(f32[256]{0:T(256)} %param.25) | copy-start | bytes 3076
  19.4 24.6 %all-to-all-start.1 = ((s32[1,32,256]{2,0,1:T(1,128)}), s32[1,32,256]{2,0,1:T(1,128)S(1)}, u32[]{:S(2)}, u32[]{:S(2)}) async-start(s32[1,32,256]{2,0,1:T(1,128)} %bitcast.39), calls=%async_computation.1 | async-start | bytes 65536 | tf_op jit(solution)/shard_map/all_to_all | solution.py:143
  44.0 14.0 %all-to-all-start = ((f32[3,32,256]{2,0,1:T(4,128)}), f32[3,32,256]{2,0,1:T(4,128)S(1)}, u32[]{:S(2)}, u32[]{:S(2)}) async-start(f32[3,32,256]{2,0,1:T(4,128)} %copy.46), calls=%async_computation | async-start | bytes 262144 | tf_op jit(solution)/shard_map/all_to_all | solution.py:150
  58.1 254.3 %copy-start.9 = (s32[256]{0:T(256)S(1)}, s32[256]{0:T(256)}, u32[]{:S(2)}) copy-start(s32[256]{0:T(256)} %param.28) | copy-start | bytes 3076
  58.1 254.3 %copy-start.6 = (f32[2048]{0:T(1024)S(1)}, f32[2048]{0:T(1024)}, u32[]{:S(2)}) copy-start(f32[2048]{0:T(1024)} %param.23) | copy-start | bytes 24580
  58.1 254.3 %copy-start.7 = (f32[2048]{0:T(1024)S(1)}, f32[2048]{0:T(1024)}, u32[]{:S(2)}) copy-start(f32[2048]{0:T(1024)} %param.21) | copy-start | bytes 24580
  58.1 254.4 %copy-start.8 = (f32[2048]{0:T(1024)S(1)}, f32[2048]{0:T(1024)}, u32[]{:S(2)}) copy-start(f32[2048]{0:T(1024)} %param.22) | copy-start | bytes 24580
  58.1 274.7 %copy-start.4 = (f32[256]{0:T(256)S(1)}, f32[256]{0:T(256)}, u32[]{:S(2)}) copy-start(f32[256]{0:T(256)} %param.26) | copy-start | bytes 3076
  58.1 274.6 %copy-start.11 = (f32[32]{0:T(128)S(1)}, f32[32]{0:T(128)}, u32[]{:S(2)}) copy-start(f32[32]{0:T(128)} %param.27) | copy-start | bytes 388
  60.8 12.0 %copy-start = (f32[1024,512]{1,0:T(8,128)S(1)}, f32[1024,512]{1,0:T(8,128)}, u32[]{:S(2)}) copy-start(f32[1024,512]{1,0:T(8,128)} %copy.73) | copy-start | bytes 6291460 | tf_op jit(solution)/shard_map/while
  92.2 12.0 %copy-start = (f32[1024,512]{1,0:T(8,128)S(1)}, f32[1024,512]{1,0:T(8,128)}, u32[]{:S(2)}) copy-start(f32[1024,512]{1,0:T(8,128)} %copy.73) | copy-start | bytes 6291460 | tf_op jit(solution)/shard_map/while
  123.6 12.0 %copy-start = (f32[1024,512]{1,0:T(8,128)S(1)}, f32[1024,512]{1,0:T(8,128)}, u32[]{:S(2)}) copy-start(f32[1024,512]{1,0:T(8,128)} %copy.73) | copy-start | bytes 6291460 | tf_op jit(solution)/shard_map/while
  155.1 12.0 %copy-start = (f32[1024,512]{1,0:T(8,128)S(1)}, f32[1024,512]{1,0:T(8,128)}, u32[]{:S(2)}) copy-start(f32[1024,512]{1,0:T(8,128)} %copy.73) | copy-start | bytes 6291460 | tf_op jit(solution)/shard_map/while
  186.5 12.0 %copy-start = (f32[1024,512]{1,0:T(8,128)S(1)}, f32[1024,512]{1,0:T(8,128)}, u32[]{:S(2)}) copy-start(f32[1024,512]{1,0:T(8,128)} %copy.73) | copy-start | bytes 6291460 | tf_op jit(solution)/shard_map/while
  217.9 12.0 %copy-start = (f32[1024,512]{1,0:T(8,128)S(1)}, f32[1024,512]{1,0:T(8,128)}, u32[]{:S(2)}) copy-start(f32[1024,512]{1,0:T(8,128)} %copy.73) | copy-start | bytes 6291460 | tf_op jit(solution)/shard_map/while
  249.3 12.0 %copy-start = (f32[1024,512]{1,0:T(8,128)S(1)}, f32[1024,512]{1,0:T(8,128)}, u32[]{:S(2)}) copy-start(f32[1024,512]{1,0:T(8,128)} %copy.73) | copy-start | bytes 6291460 | tf_op jit(solution)/shard_map/while
  280.8 12.0 %copy-start = (f32[1024,512]{1,0:T(8,128)S(1)}, f32[1024,512]{1,0:T(8,128)}, u32[]{:S(2)}) copy-start(f32[1024,512]{1,0:T(8,128)} %copy.73) | copy-start | bytes 6291460 | tf_op jit(solution)/shard_map/while
  309.5 12.6 %all-to-all-start.2 = ((f32[5,32,256]{2,0,1:T(8,128)}), f32[5,32,256]{2,0,1:T(8,128)S(1)}, u32[]{:S(2)}, u32[]{:S(2)}) async-start(f32[5,32,256]{2,0,1:T(8,128)} %bitcast.41), calls=%async_computation.2 | async-start | bytes 524288 | tf_op jit(solution)/shard_map/all_to_all | solution.py:162
  312.1 407.1 %all-reduce.3.cloned.1.call-start = ((), (), s32[]{:S(2)}) async-start(), calls=%async_computation.3 | async-start | bytes 524288
  332.8 386.4 %copy-start.5 = (f32[2,32,8]{1,2,0:T(8,128)S(1)}, f32[2,32,8]{1,2,0:T(8,128)}, u32[]{:S(2)}) copy-start(f32[2,32,8]{1,2,0:T(8,128)} %param.29) | copy-start | bytes 6148
  593.6 0.7 copy-start.2
Sparse Core Ops, SparseCore 0:
  594.4 124.7 all-reduce.2
where the time goes:
time: 728 us; the launch traced here: 727 us
  other arithmetic  388 us (53%)
  local copies, waits for them, and re-layouts  166 us (23%)
  waiting for transfers between devices  142 us (20%)
  starting transfers between devices  16 us (2%)
  between operations  14.4 us (2%)
    reduce_sum x8, other arithmetic, spectra_terms(): cos_sum = jnp.sum(amplitude[:, :, None] * jnp.cos(phases), axis=0).T  249 us
    while x8, other arithmetic  127 us
    unnamed x2, waiting for transfers between devices  124 us
    gather x8, local copies, waits for them, and re-layouts, sample(): gathered = jnp.take(fields, pieces[0], axis=0).astype(jnp.float32)  96.2 us
    while x24, local copies, waits for them, and re-layouts  14.7 us
  transfers between devices with their start and end apart: 4, of which 3 were waited for; matrix products, arithmetic and copies ran while one was open for 3% of the time, Pallas kernels for 0%

commit v1 on v0

v1 whole, which is shorter than its diff:
```python
import functools
import math

import jax
import jax.numpy as jnp
import numpy as np
from jax import lax
from jax.experimental import pallas as pl
from jax.experimental.pallas import tpu as pltpu
from jax.sharding import PartitionSpec as P

FIELDS = 5
AXES = ("gx", "gy")
F32 = jnp.float32
BF16 = jnp.bfloat16
BASIS = 8

gll_nodes = np.array(
    [
        -1.0,
        -0.8717401485096066,
        -0.5917001814331423,
        -0.2092992179024789,
        0.2092992179024789,
        0.5917001814331423,
        0.8717401485096066,
        1.0,
    ]
)
gll_scale = np.array(
    [1.0 / np.prod([gll_nodes[i] - gll_nodes[m] for m in range(8) if m != i]) for i in range(8)]
)
omega_base = 0.25


def three_parts(x):
    high = x.astype(BF16)
    rest = x - high.astype(F32)
    middle = rest.astype(BF16)
    low = (rest - middle.astype(F32)).astype(BF16)
    return high, middle, low


def contract_last(a, b):
    return lax.dot_general(a, b, (((1,), (1,)), ((), ())), preferred_element_type=F32)


def pack_kernel(devices, cap, target_ref, ids_ref, coords_ref, send_ref, rank_ref):
    points = target_ref.shape[1]
    width = math.gcd(points, 512)
    before = (
        lax.broadcasted_iota(jnp.int32, (width, width), 0)
        < lax.broadcasted_iota(jnp.int32, (width, width), 1)
    )
    before = jnp.where(before, 1.0, 0.0).astype(BF16)
    offset = jnp.zeros((devices, 1), F32)
    sums = [jnp.zeros((devices, cap), F32) for _ in range(4)]
    for block in range(points // width):
        lanes = slice(block * width, (block + 1) * width)
        mine = target_ref[:, lanes] == lax.broadcasted_iota(jnp.int32, (devices, width), 0)
        hot = jnp.where(mine, 1.0, 0.0)
        hot_half = hot.astype(BF16)
        within = jnp.dot(hot_half, before, preferred_element_type=F32) + offset
        rank = jnp.sum(hot * within, axis=0, keepdims=True).astype(jnp.int32)
        offset = offset + jnp.sum(hot, axis=1, keepdims=True)
        rank_ref[:, lanes] = rank
        spot = jnp.where(lax.broadcasted_iota(jnp.int32, (cap, width), 0) == rank, 1.0, 0.0)
        spot = spot.astype(BF16)
        for entry in range(4):
            if entry == 0:
                row = ids_ref[:, lanes].astype(F32)
            else:
                row = coords_ref[entry - 1 : entry, lanes]
            for part in three_parts(row * hot):
                sums[entry] = sums[entry] + contract_last(part, spot)
    for entry in range(4):
        send_ref[:, entry, :] = sums[entry]


def interp_kernel(ids_ref, recv_ref, expand_ref, fields_ref, out_ref, table, weights):
    devices, _, cap = recv_ref.shape
    block = min(cap, 128)
    elements = fields_ref.shape[0]

    def widen(e, carry):
        table[e, 0:FIELDS, :] = fields_ref[e].astype(F32)
        return carry

    lax.fori_loop(0, elements, widen, 0, unroll=8)
    node = lax.broadcasted_iota(jnp.int32, (8, block), 0)
    lane = lax.broadcasted_iota(jnp.int32, (FIELDS, block), 1)
    scale = jnp.zeros((8, block), F32)
    for i in range(8):
        scale = jnp.where(node == i, float(gll_scale[i]), scale)

    def source(s, carry):
        for half in range(cap // block):
            lanes = slice(half * block, (half + 1) * block)
            bases = []
            for axis in range(3):
                x = recv_ref[s, axis + 1 : axis + 2, lanes]
                product = scale
                for m in range(8):
                    product = product * jnp.where(node == m, 1.0, x - float(gll_nodes[m]))
                bases.append(product)
            stacked = jnp.concatenate(bases, axis=0)
            parts = jnp.concatenate([p.astype(F32) for p in three_parts(stacked)], axis=0)
            parts = parts.T.astype(BF16)
            wide = jnp.dot(parts, expand_ref[...], preferred_element_type=F32)
            pair = wide[:, 512:640] * wide[:, 640:768]
            for quarter in range(4):
                columns = slice(quarter * 128, (quarter + 1) * 128)
                weights[half, :, columns] = wide[:, columns] * pair
            result = jnp.zeros((FIELDS, block), F32)
            for p in range(block):
                e = ids_ref[s * cap + half * block + p]
                total = None
                for quarter in range(4):
                    columns = slice(quarter * 128, (quarter + 1) * 128)
                    term = table[e, 0:FIELDS, columns] * weights[half, p : p + 1, columns]
                    total = term if total is None else total + term
                value = jnp.sum(total, axis=1, keepdims=True)
                result = jnp.where(lane == p, value, result)
            out_ref[s, :, lanes] = result
        return carry

    lax.fori_loop(0, devices, source, 0)


def sincos(angle):
    turns = jnp.floor(angle * float(2.0 / math.pi) + 0.5)
    r = angle - turns * 1.5703125
    r = r - turns * 4.837512969970703125e-4
    r = r - turns * 7.54978995489188e-8
    z = r * r
    sine = ((-1.9515295891e-4 * z + 8.3321608736e-3) * z - 1.6666654611e-1) * z * r + r
    cosine = (
        (2.443315711809948e-5 * z - 1.388731625493765e-3) * z + 4.166664568298827e-2
    ) * z * z + (1.0 - 0.5 * z)
    quadrant = turns.astype(jnp.int32)
    odd = (quadrant & 1) == 1
    first = jnp.where(odd, sine, cosine)
    second = jnp.where(odd, cosine, sine)
    first = jnp.where(((quadrant + 1) & 2) == 2, -first, first)
    second = jnp.where((quadrant & 2) == 2, -second, second)
    return first, second


def spectra_kernel(
    norm_scale,
    replies_ref,
    target_ref,
    rank_ref,
    point_ref,
    obs_x_ref,
    obs_y_ref,
    obs_z_ref,
    surface_ref,
    sums_ref,
    rows,
    acc,
):
    devices, _, cap = replies_ref.shape
    points = target_ref.shape[1]
    width = math.gcd(points, 512)
    parts = [three_parts(replies_ref[:, f, :]) for f in range(FIELDS)]
    stacked = jnp.concatenate([p for triple in parts for p in triple], axis=0)
    for block in range(points // width):
        lanes = slice(block * width, (block + 1) * width)
        mine = target_ref[:, lanes] == lax.broadcasted_iota(jnp.int32, (devices, width), 0)
        spot = jnp.where(
            lax.broadcasted_iota(jnp.int32, (cap, width), 0) == rank_ref[:, lanes], 1.0, 0.0
        ).astype(BF16)
        found = jnp.dot(stacked, spot, preferred_element_type=F32)
        found = found.reshape(FIELDS, 3, devices, width)
        values = []
        for f in range(FIELDS):
            whole = (found[f, 0] + found[f, 1]) + found[f, 2]
            value = jnp.sum(jnp.where(mine, whole, 0.0), axis=0, keepdims=True)
            surface_ref[f : f + 1, lanes] = value
            values.append(value)
        density, vel_x, vel_y, vel_z, pressure = values
        cos_p = point_ref[0:1, lanes]
        sin_p = point_ref[1:2, lanes]
        weight = point_ref[3:4, lanes] * norm_scale
        flux = weight * density * (vel_x * cos_p + vel_y * sin_p)
        push = weight * pressure
        for at, row in enumerate(
            (
                cos_p,
                sin_p,
                point_ref[2:3, lanes],
                flux,
                push * cos_p + flux * vel_x,
                push * sin_p + flux * vel_y,
                flux * vel_z,
            )
        ):
            rows[at, :, lanes] = jnp.broadcast_to(row, (8, width))

    group = 4
    tile = 128 * group
    lane = lax.broadcasted_iota(jnp.int32, (8, 128), 1)

    def add_up(terms):
        while len(terms) > 1:
            terms = [a + b for a, b in zip(terms[0::2], terms[1::2])]
        return terms[0]

    def observers(g, carry):
        at = pl.ds(pl.multiple_of(g * 8, 8), 8)
        obs_x, obs_y, obs_z = obs_x_ref[at, :], obs_y_ref[at, :], obs_z_ref[at, :]
        for part in range(points // tile):
            state = []
            for u in range(group):
                lanes = slice(part * tile + u * 128, part * tile + (u + 1) * 128)
                dx = obs_x - rows[0, :, lanes]
                dy = obs_y - rows[1, :, lanes]
                dz = obs_z - rows[2, :, lanes]
                square = dx * dx + dy * dy + dz * dz
                inverse = lax.rsqrt(square)
                rough = square * inverse
                half = 0.5 * inverse
                dist = rough + half * (square - rough * rough)
                inverse = inverse + inverse * (0.5 - half * (square * inverse))
                along = dx * rows[4, :, lanes] + dy * rows[5, :, lanes] + dz * rows[6, :, lanes]
                amp = inverse * (rows[3, :, lanes] + inverse * along)
                c1, s1 = sincos(dist * omega_base)
                c2, s2 = c1 * c1 - s1 * s1, 2.0 * c1 * s1
                c4, s4 = c2 * c2 - s2 * s2, 2.0 * c2 * s2
                c8, s8 = c4 * c4 - s4 * s4, 2.0 * c4 * s4
                c16, s16 = c8 * c8 - s8 * s8, 2.0 * c8 * s8
                c24 = c16 * c8 - s16 * s8
                state.append(
                    [amp, jnp.zeros_like(amp), amp * c1, amp * s1, 2.0 * c1, 2.0 * c8, 2.0 * c16, 2.0 * c24]
                )

            def put(column, terms):
                total = add_up(terms)
                if part > 0:
                    total = total + acc[column]
                acc[column] = total

            put(8 * BASIS, [one[0] for one in state])
            for n in range(BASIS):
                for trig in range(2):
                    now = [one[2 + trig] for one in state]
                    put(4 * BASIS * trig + n, now)
                    for multiple in range(3):
                        put(
                            4 * BASIS * trig + BASIS * (multiple + 1) + n,
                            [value * one[5 + multiple] for value, one in zip(now, state)],
                        )
                for one in state:
                    c_next = one[4] * one[2] - one[0]
                    s_next = one[4] * one[3] - one[1]
                    one[0], one[1], one[2], one[3] = one[2], one[3], c_next, s_next
        result = jnp.zeros((8, 128), F32)
        for column in range(8 * BASIS + 1):
            result = jnp.where(lane == column, jnp.sum(acc[column], axis=1, keepdims=True), result)
        sums_ref[at, :] = result
        return carry

    lax.fori_loop(0, obs_x_ref.shape[0] // 8, observers, 0)


def expansion():
    spread = np.zeros((24, 768), np.float32)
    for q in range(512):
        spread[q // 64, q] = 1.0
    for lane in range(128):
        spread[8 + (lane // 8) % 8, 512 + lane] = 1.0
        spread[16 + lane % 8, 640 + lane] = 1.0
    return np.concatenate([spread] * 3, axis=0)


def recombination():
    rows = np.zeros((128, 64), np.float32)
    cos_of, sin_of = {}, {}
    unit = np.eye(128, dtype=np.float32)
    cos_of[0], sin_of[0] = unit[8 * BASIS], np.zeros(128, np.float32)
    for n in range(1, BASIS + 1):
        cos_of[n], sin_of[n] = unit[n - 1], unit[4 * BASIS + n - 1]
    for multiple in (1, 2, 3):
        m = multiple * BASIS
        for n in range(1, BASIS + 1):
            cos_of[m + n] = unit[multiple * BASIS + n - 1] - cos_of[m - n]
            sin_of[m + n] = unit[4 * BASIS + multiple * BASIS + n - 1] + sin_of[m - n]
    for k in range(32):
        rows[:, k] = cos_of[k + 1]
        rows[:, 32 + k] = sin_of[k + 1]
    return rows


def on_device(
    element_fields,
    ref_coords,
    local_element,
    owner,
    point_angle,
    point_axial,
    panel_weight,
    obs_radius,
    obs_angle,
    obs_axial,
    step_phase,
    observer_slot,
    prior_spectra,
):
    devices = lax.axis_size(AXES)
    points = local_element.shape[0]
    cap = 4 * points // devices
    observers = obs_radius.shape[0]
    harmonics = step_phase.shape[0]
    norm_scale = 1.0 / math.sqrt(points * devices)
    target = owner.reshape(1, points)

    send, rank = pl.pallas_call(
        functools.partial(pack_kernel, devices, cap),
        out_shape=(
            jax.ShapeDtypeStruct((devices, 4, cap), F32),
            jax.ShapeDtypeStruct((1, points), jnp.int32),
        ),
        name="pack",
    )(target, local_element.reshape(1, points), ref_coords)
    recv = lax.all_to_all(send, AXES, split_axis=0, concat_axis=0, tiled=True)
    ids = recv[:, 0, :].reshape(devices * cap).astype(jnp.int32)
    vmem = pl.BlockSpec(memory_space=pltpu.VMEM)
    served = pl.pallas_call(
        interp_kernel,
        out_shape=jax.ShapeDtypeStruct((devices, FIELDS, cap), F32),
        in_specs=[pl.BlockSpec(memory_space=pltpu.SMEM), vmem, vmem, vmem],
        out_specs=vmem,
        scratch_shapes=[
            pltpu.VMEM((element_fields.shape[0], 8, 512), F32),
            pltpu.VMEM((max(1, cap // 128), min(cap, 128), 512), F32),
        ],
        name="interp",
    )(ids, recv, jnp.asarray(expansion(), BF16), element_fields)
    replies = lax.all_to_all(served, AXES, split_axis=0, concat_axis=0, tiled=True)

    chosen = observer_slot[:, None] == jnp.arange(observers, dtype=jnp.int32)[None, :]
    in_order = lambda x: jnp.sum(jnp.where(chosen, x[:, None], 0.0), axis=0)
    radius = in_order(obs_radius)
    obs_x = in_order(obs_radius * jnp.cos(obs_angle))
    obs_y = in_order(obs_radius * jnp.sin(obs_angle))
    obs_z = in_order(obs_axial)
    spread = lambda x: jnp.broadcast_to(x[:, None], (observers, 128))
    point_rows = jnp.stack([jnp.cos(point_angle), jnp.sin(point_angle), point_axial, panel_weight])
    surface_values, sums = pl.pallas_call(
        functools.partial(spectra_kernel, norm_scale),
        out_shape=(
            jax.ShapeDtypeStruct((FIELDS, points), F32),
            jax.ShapeDtypeStruct((observers, 128), F32),
        ),
        scratch_shapes=[
            pltpu.VMEM((7, 8, points), F32),
            pltpu.VMEM((8 * BASIS + 1, 8, 128), F32),
        ],
        name="spectra",
    )(replies, target, rank, point_rows, spread(obs_x), spread(obs_y), spread(obs_z))

    own = observers // devices
    gathered = lax.all_to_all(sums, AXES, split_axis=0, concat_axis=0, tiled=True)
    summed = jnp.sum(gathered.reshape(devices, own, 128), axis=0)
    me = lax.axis_index(AXES)
    own_radius = lax.dynamic_slice(radius, (me * own,), (own,))
    recombined = jnp.dot(
        summed * own_radius[:, None], jnp.asarray(recombination()), precision=lax.Precision.HIGHEST
    )
    cos_sum, sin_sum = recombined[:, :harmonics].T, recombined[:, harmonics:].T
    cos_f, sin_f = jnp.cos(step_phase)[:, None], jnp.sin(step_phase)[:, None]
    terms = jnp.stack([cos_f * cos_sum - sin_f * sin_sum, -(sin_f * cos_sum + cos_f * sin_sum)])
    return (surface_values, prior_spectra + terms)


def solution(mesh):
    return jax.shard_map(
        on_device,
        mesh=mesh,
        in_specs=(
            P(AXES, None, None),
            P(None, AXES),
            P(AXES),
            P(AXES, None),
            P(AXES),
            P(AXES),
            P(AXES),
            P(),
            P(),
            P(),
            P(),
            P(),
            P(None, None, AXES),
        ),
        out_specs=(P(None, AXES), P(None, None, AXES)),
        check_vma=False,
    )
```

time: 728 us -> 108 us (0.15)
  other arithmetic: 388 us -> 3.01 us
  local copies, waits for them, and re-layouts: 166 us -> 7.83 us
  waiting for transfers between devices: 142 us -> 19 us
  Pallas kernels: 0 us -> 62.2 us
  between operations: 14.4 us -> 0.78 us
    reduce_sum x9 -> x2, other arithmetic: 249 us -> 0.29 us  [the longest x1 0.25 us: on_device(): in_order = lambda x: jnp.sum(jnp.where(chosen, x[:, None], 0.0), axis=0)]
    while x8 -> x0, other arithmetic: 127 us -> none
    unnamed x2 -> x0, waiting for transfers between devices: 124 us -> none
    gather x9 -> x0, local copies, waits for them, and re-layouts: 104 us -> none  [the longest x8 96.2 us: sample(): gathered = jnp.take(fields, pieces[0], axis=0).astype(jnp.float32)]
    pallas_call x0 -> x3, Pallas kernels: none -> 62.2 us  [the longest x1 31.5 us: on_device(): pl.pallas_call(interp_kernel, out_shape=jax.ShapeDtypeStruct((devices, FI...]
    scatter x3 -> x0, local copies, waits for them, and re-layouts: 23.9 us -> none  [the longest x1 8.8 us: on_device(): jnp.zeros((devices * capacity,), jnp.int32).at[position].set(local_element)]
    while x26 -> x0, local copies, waits for them, and re-layouts: 18.5 us -> none
  transfers between devices with their start and end apart: 4 -> 3, of which waited for: 3 -> 3; matrix products, arithmetic and copies ran while one was open for 3% -> 7% of each run, Pallas kernels for 0% -> 0%
where the time goes in v1:
time: 108 us; the launch traced here: 107 us
  Pallas kernels  62.2 us (58%)
  waiting for transfers between devices  19 us (18%)
  starting transfers between devices  14.1 us (13%)
  local copies, waits for them, and re-layouts  7.83 us (7%)
  other arithmetic  3.01 us (3%)
    pallas_call x1, Pallas kernels, on_device(): pl.pallas_call(interp_kernel, out_shape=jax.ShapeDtypeStruct((devices, FI...  31.5 us
    pallas_call x1, Pallas kernels, on_device(): pl.pallas_call(functools.partial(spectra_kernel, norm_scale), out_shape=(...  24.8 us
    all_to_all x1, waiting for transfers between devices, on_device(): lax.all_to_all(served, AXES, split_axis=0, concat_axis=0, tiled=True)  9.06 us
    all_to_all x1, waiting for transfers between devices, on_device(): lax.all_to_all(sums, AXES, split_axis=0, concat_axis=0, tiled=True)  8.03 us
    all_to_all x1, starting transfers between devices, on_device(): recv = lax.all_to_all(send, AXES, split_axis=0, concat_axis=0, tiled=True)  7.33 us
    pallas_call x1, Pallas kernels, on_device(): pl.pallas_call(functools.partial(pack_kernel, devices, cap), out_shape=(j...  5.84 us
    unnamed x23, local copies, waits for them, and re-layouts  5.44 us
    all_to_all x1, starting transfers between devices, on_device(): lax.all_to_all(served, AXES, split_axis=0, concat_axis=0, tiled=True)  3.94 us
  transfers between devices with their start and end apart: 3, of which 3 were waited for; matrix products, arithmetic and copies ran while one was open for 7% of the time, Pallas kernels for 0%

profile of v1, /device:TPU:0, one launch (start us, length us, event | category | flops | bytes accessed | tf_op | source)
XLA Modules:
  0.0 107.1 jit_solution(10075796401635267990)
XLA Ops:
  0.6 0.0 copy-start.3
  0.6 5.8 %pack.1 = (f32[32,4,256]{2,1,0:T(4,128)}, s32[1,2048]{1,0:T(1,128)}) custom-call(s32[1,2048]{1,0:T(1,128)} %bitcast.19, s32[1,2048]{1,0:T(1,128)} %bitcast.23, f32[3,2048]{1,0:T(4,128)} %coords_ref.1), custom_call_target="tpu_custom_call" | custom-call | tf_op jit(solution)/shard_map/pack/pallas_call | solution.py:318
  6.5 7.3 %all-to-all-start = ((f32[32,4,256]{2,1,0:T(4,128)}), f32[32,4,256]{2,1,0:T(4,128)S(1)}, u32[]{:S(2)}, u32[]{:S(2)}) async-start(f32[32,4,256]{2,1,0:T(4,128)} %get-tuple-element.6), calls=%async_computation | async-start | bytes 262144 | tf_op jit(solution)/shard_map/all_to_all | solution.py:326
  13.8 0.7 cosine_multiply_fusion
  14.6 5.4 %copy.18.fields_ref = bf16[512,5,512]{2,1,0:T(8,128)(2,1)} copy(bf16[512,5,512]{2,0,1:T(8,128)(2,1)} %param.15) | data formatting | bytes 5242880 | tf_op args[0]
  19.9 0.0 copy-done.3
  20.0 0.0 copy-start.5
  20.0 0.0 copy-start.6
  20.0 0.0 copy-start.10
  20.0 0.0 copy-start.2
  20.0 0.0 copy-start.4
  20.1 1.9 %all-to-all-done.recv_ref = f32[32,4,256]{2,1,0:T(4,128)S(1)} async-done(((f32[32,4,256]{2,1,0:T(4,128)}), f32[32,4,256]{2,1,0:T(4,128)S(1)}, u32[]{:S(2)}, u32[]{:S(2)}) %all-to-all-start) | async-done | bytes 131104 | tf_op jit(solution)/shard_map/all_to_all | solution.py:326
  22.0 0.7 slice_convert_fusion
  22.6 0.0 copy-done.1
  22.6 31.5 %interp.1 = f32[32,5,256]{2,1,0:T(8,128)} custom-call(s32[8192]{0:T(1024)} %bitcast.17, f32[32,4,256]{2,1,0:T(4,128)} %copy-done.1, bf16[72,768]{1,0:T(8,128)(2,1)} %constant.20.clone.expand_ref, bf16[512,5,512]{2,1,0:T(8,128)(2,1)} %copy.18.fields_ref), custom_call_target="tpu_custom_call" | custom-call | tf_op jit(solution)/shard_map/interp/pallas_call | solution.py:329
  54.2 3.9 %all-to-all-start.1 = ((f32[32,5,256]{2,1,0:T(8,128)}), f32[32,5,256]{2,1,0:T(8,128)S(1)}, u32[]{:S(2)}, u32[]{:S(2)}) async-start(f32[32,5,256]{2,1,0:T(8,128)} %interp.1), calls=%async_computation.1 | async-start | bytes 524288 | tf_op jit(solution)/shard_map/all_to_all | solution.py:340
  58.1 0.0 copy-done.7
  58.1 0.0 copy-done.8
  58.1 0.0 copy-done.9
  58.2 0.2 select_reduce_fusion
  58.4 0.6 pad_maximum_fusion.point_ref
  59.1 9.1 %all-to-all-done.1.replies_ref = f32[32,5,256]{2,1,0:T(8,128)S(1)} async-done(((f32[32,5,256]{2,1,0:T(8,128)}), f32[32,5,256]{2,1,0:T(8,128)S(1)}, u32[]{:S(2)}, u32[]{:S(2)}) %all-to-all-start.1) | async-done | bytes 163872 | tf_op jit(solution)/shard_map/all_to_all | solution.py:340
  68.1 0.7 broadcast_in_dim.59.obs_x_ref
  68.9 0.8 broadcast_in_dim.61.obs_y_ref
  69.6 0.7 broadcast_in_dim.63.obs_z_ref
  70.4 24.8 %spectra.1 = (f32[5,2048]{1,0:T(8,128)}, f32[256,128]{1,0:T(8,128)}) custom-call(f32[32,5,256]{2,1,0:T(8,128)} %copy-done, s32[1,2048]{1,0:T(1,128)} %bitcast.20, s32[1,2048]{1,0:T(1,128)} %get-tuple-element.7.rank_ref, f32[4,2048]{1,0:T(4,128)} %pad_maximum_fusion.point_ref, f32[256,128]{1,0:T(8,128)} %broadcast_in_dim.59.obs_x_ref, ...), custom_call_target="tpu_custom_call" | custom-call | tf_op jit(solution)/shard_map/spectra/pallas_call | solution.py:350
  95.2 2.9 %all-to-all-start.2 = ((f32[32,8,128]{2,1,0:T(8,128)}), f32[32,8,128]{2,1,0:T(8,128)S(1)}, u32[]{:S(2)}, u32[]{:S(2)}) async-start(f32[32,8,128]{2,1,0:T(8,128)} %bitcast.18), calls=%async_computation.2 | async-start | bytes 262144 | tf_op jit(solution)/shard_map/all_to_all | solution.py:364
  98.0 0.1 dynamic_slice.3
  98.1 8.0 %all-to-all-done.2 = f32[32,8,128]{2,1,0:T(8,128)S(1)} async-done(((f32[32,8,128]{2,1,0:T(8,128)}), f32[32,8,128]{2,1,0:T(8,128)S(1)}, u32[]{:S(2)}, u32[]{:S(2)}) %all-to-all-start.2) | async-done | bytes 131104 | tf_op jit(solution)/shard_map/all_to_all | solution.py:364
  106.2 0.2 fusion
  106.4 0.1 subtract_bitcast_fusion
  106.5 0.6 maximum_add_fusion
  (14 shorter events, 0.1 us)
Async XLA Ops:
  0.6 19.3 %copy-start.3 = (f32[2048]{0:T(1024)S(1)}, f32[2048]{0:T(1024)}, u32[]{:S(2)}) copy-start(f32[2048]{0:T(1024)} %param.19) | copy-start | bytes 24580
  6.5 15.5 %all-to-all-start = ((f32[32,4,256]{2,1,0:T(4,128)}), f32[32,4,256]{2,1,0:T(4,128)S(1)}, u32[]{:S(2)}, u32[]{:S(2)}) async-start(f32[32,4,256]{2,1,0:T(4,128)} %get-tuple-element.6), calls=%async_computation | async-start | bytes 262144 | tf_op jit(solution)/shard_map/all_to_all | solution.py:326
  19.9 38.2 %copy-start.7 = (f32[256]{0:T(256)S(1)}, f32[256]{0:T(256)}, u32[]{:S(2)}) copy-start(f32[256]{0:T(256)} %param.22) | copy-start | bytes 3076
  19.9 38.2 %copy-start.8 = (s32[256]{0:T(256)S(1)}, s32[256]{0:T(256)}, u32[]{:S(2)}) copy-start(s32[256]{0:T(256)} %param.26) | copy-start | bytes 3076
  19.9 38.2 %copy-start.9 = (f32[256]{0:T(256)S(1)}, f32[256]{0:T(256)}, u32[]{:S(2)}) copy-start(f32[256]{0:T(256)} %param.24) | copy-start | bytes 3076
  20.0 38.5 %copy-start.5 = (f32[2048]{0:T(1024)S(1)}, f32[2048]{0:T(1024)}, u32[]{:S(2)}) copy-start(f32[2048]{0:T(1024)} %param.21) | copy-start | bytes 24580
  20.0 38.5 %copy-start.6 = (f32[2048]{0:T(1024)S(1)}, f32[2048]{0:T(1024)}, u32[]{:S(2)}) copy-start(f32[2048]{0:T(1024)} %param.20) | copy-start | bytes 24580
  20.0 78.1 %copy-start.10 = (f32[32]{0:T(128)S(1)}, f32[32]{0:T(128)}, u32[]{:S(2)}) copy-start(f32[32]{0:T(128)} %param.25) | copy-start | bytes 388
  20.0 86.2 %copy-start.2 = (f32[128,64]{1,0:T(8,128)S(1)}, f32[128,64]{1,0:T(8,128)}, u32[]{:S(2)}) copy-start(f32[128,64]{1,0:T(8,128)} %constant.21.clone) | copy-start | bytes 98308
  20.0 86.5 %copy-start.4 = (f32[2,32,8]{1,2,0:T(8,128)S(1)}, f32[2,32,8]{1,2,0:T(8,128)}, u32[]{:S(2)}) copy-start(f32[2,32,8]{1,2,0:T(8,128)} %param.27) | copy-start | bytes 6148
  22.0 0.7 copy-start.1
  54.2 14.0 %all-to-all-start.1 = ((f32[32,5,256]{2,1,0:T(8,128)}), f32[32,5,256]{2,1,0:T(8,128)S(1)}, u32[]{:S(2)}, u32[]{:S(2)}) async-start(f32[32,5,256]{2,1,0:T(8,128)} %interp.1), calls=%async_computation.1 | async-start | bytes 524288 | tf_op jit(solution)/shard_map/all_to_all | solution.py:340
  68.1 2.2 %copy-start = (f32[32,5,256]{2,1,0:T(8,128)}, f32[32,5,256]{2,1,0:T(8,128)S(1)}, u32[]{:S(2)}) copy-start(f32[32,5,256]{2,1,0:T(8,128)S(1)} %all-to-all-done.1.replies_ref) | copy-start | bytes 491524
  95.2 11.0 %all-to-all-start.2 = ((f32[32,8,128]{2,1,0:T(8,128)}), f32[32,8,128]{2,1,0:T(8,128)S(1)}, u32[]{:S(2)}, u32[]{:S(2)}) async-start(f32[32,8,128]{2,1,0:T(8,128)} %bitcast.18), calls=%async_computation.2 | async-start | bytes 262144 | tf_op jit(solution)/shard_map/all_to_all | solution.py:364

commit v2 on v1

--- a/solution.py
+++ b/solution.py
@@ -45,7 +45,72 @@
     return lax.dot_general(a, b, (((1,), (1,)), ((), ())), preferred_element_type=F32)
 
 
-def pack_kernel(devices, cap, target_ref, ids_ref, coords_ref, send_ref, rank_ref):
+def where_am_i():
+    return lax.axis_index(AXES)
+
+
+def place_of(device):
+    inner = lax.axis_size("gy")
+    return (device // inner, lax.rem(device, inner))
+
+
+def greet(devices):
+    me = where_am_i()
+    barrier = pltpu.get_barrier_semaphore()
+
+    def signal(step, carry):
+        other = lax.rem(me + step, devices)
+        pl.semaphore_signal(
+            barrier, inc=1, device_id=place_of(other), device_id_type=pl.DeviceIdType.MESH
+        )
+        return carry
+
+    lax.fori_loop(1, devices, signal, 0)
+
+
+def met(devices):
+    pl.semaphore_wait(pltpu.get_barrier_semaphore(), devices - 1)
+
+
+def transfer(stage, landing, send_sems, recv_sems, other, sender):
+    return pltpu.make_async_remote_copy(
+        src_ref=stage.at[other],
+        dst_ref=landing.at[sender],
+        send_sem=send_sems.at[other],
+        recv_sem=recv_sems.at[sender],
+        device_id=place_of(other),
+        device_id_type=pl.DeviceIdType.MESH,
+    )
+
+
+def finish(devices, stage, landing, send_sems, recv_sems):
+    me = where_am_i()
+
+    def wait(step, carry):
+        other = lax.rem(me + step, devices)
+        transfer(stage, landing, send_sems, recv_sems, other, me).wait_send()
+        transfer(stage, landing, send_sems, recv_sems, other, other).wait_recv()
+        return carry
+
+    lax.fori_loop(1, devices, wait, 0)
+
+
+def pack_kernel(
+    devices,
+    cap,
+    target_ref,
+    ids_ref,
+    coords_ref,
+    recv_ref,
+    served_ids_ref,
+    rank_ref,
+    send_ref,
+    landing,
+    send_sems,
+    recv_sems,
+):
+    greet(devices)
+    me = where_am_i()
     points = target_ref.shape[1]
     width = math.gcd(points, 512)
     before = (
@@ -75,25 +140,55 @@
                 sums[entry] = sums[entry] + contract_last(part, spot)
     for entry in range(4):
         send_ref[:, entry, :] = sums[entry]
-
-
-def interp_kernel(ids_ref, recv_ref, expand_ref, fields_ref, out_ref, table, weights):
+    met(devices)
+
+    def begin(step, carry):
+        other = lax.rem(me + step, devices)
+        transfer(send_ref, landing, send_sems, recv_sems, other, me).start()
+        return carry
+
+    lax.fori_loop(1, devices, begin, 0)
+    landing[me] = send_ref[me]
+    finish(devices, send_ref, landing, send_sems, recv_sems)
+    recv_ref[...] = landing[...]
+    served_ids_ref[...] = landing[:, 0, :].astype(jnp.int32)
+
+
+def interp_kernel(
+    ids_ref,
+    recv_ref,
+    expand_ref,
+    fields_ref,
+    out_ref,
+    table,
+    weights_even,
+    weights_odd,
+    stage,
+    landing,
+    send_sems,
+    recv_sems,
+):
     devices, _, cap = recv_ref.shape
+    greet(devices)
+    me = where_am_i()
     block = min(cap, 128)
-    elements = fields_ref.shape[0]
-
-    def widen(e, carry):
-        table[e, 0:FIELDS, :] = fields_ref[e].astype(F32)
+    elements = fields_ref.shape[1]
+    chunk = math.gcd(elements, 16)
+
+    def widen(step, carry):
+        rows = pl.ds(pl.multiple_of(step * chunk, chunk), chunk)
+        for f in range(FIELDS):
+            table[rows, f, :] = fields_ref[f, rows, :].astype(F32)
         return carry
 
-    lax.fori_loop(0, elements, widen, 0, unroll=8)
+    lax.fori_loop(0, elements // chunk, widen, 0)
     node = lax.broadcasted_iota(jnp.int32, (8, block), 0)
     lane = lax.broadcasted_iota(jnp.int32, (FIELDS, block), 1)
     scale = jnp.zeros((8, block), F32)
     for i in range(8):
         scale = jnp.where(node == i, float(gll_scale[i]), scale)
 
-    def source(s, carry):
+    def fill(weights, s):
         for half in range(cap // block):
             lanes = slice(half * block, (half + 1) * block)
             bases = []
@@ -111,9 +206,13 @@
             for quarter in range(4):
                 columns = slice(quarter * 128, (quarter + 1) * 128)
                 weights[half, :, columns] = wide[:, columns] * pair
+
+    def evaluate(weights, s):
+        for half in range(cap // block):
+            lanes = slice(half * block, (half + 1) * block)
             result = jnp.zeros((FIELDS, block), F32)
             for p in range(block):
-                e = ids_ref[s * cap + half * block + p]
+                e = ids_ref[s, half * block + p]
                 total = None
                 for quarter in range(4):
                     columns = slice(quarter * 128, (quarter + 1) * 128)
@@ -121,10 +220,33 @@
                     total = term if total is None else total + term
                 value = jnp.sum(total, axis=1, keepdims=True)
                 result = jnp.where(lane == p, value, result)
-            out_ref[s, :, lanes] = result
+            stage[s, :, lanes] = result
+
+    def at_step(step):
+        return lax.rem(me + 1 + step, devices)
+
+    fill(weights_even, at_step(0))
+    met(devices)
+
+    def two_sources(pair_step, carry):
+        first, second = at_step(2 * pair_step), at_step(2 * pair_step + 1)
+        third = at_step(2 * pair_step + 2)
+        fill(weights_odd, second)
+        evaluate(weights_even, first)
+        transfer(stage, landing, send_sems, recv_sems, first, me).start()
+        fill(weights_even, third)
+        evaluate(weights_odd, second)
+
+        @pl.when(2 * pair_step + 1 < devices - 1)
+        def _():
+            transfer(stage, landing, send_sems, recv_sems, second, me).start()
+
         return carry
 
-    lax.fori_loop(0, devices, source, 0)
+    lax.fori_loop(0, devices // 2, two_sources, 0)
+    landing[me] = stage[me]
+    finish(devices, stage, landing, send_sems, recv_sems)
+    out_ref[...] = landing[...]
 
 
 def sincos(angle):
@@ -152,15 +274,20 @@
     target_ref,
     rank_ref,
     point_ref,
-    obs_x_ref,
-    obs_y_ref,
-    obs_z_ref,
+    obs_ref,
+    slot_ref,
     surface_ref,
     sums_ref,
     rows,
     acc,
+    stage,
+    landing,
+    send_sems,
+    recv_sems,
 ):
     devices, _, cap = replies_ref.shape
+    greet(devices)
+    me = where_am_i()
     points = target_ref.shape[1]
     width = math.gcd(points, 512)
     parts = [three_parts(replies_ref[:, f, :]) for f in range(FIELDS)]
@@ -180,16 +307,15 @@
             surface_ref[f : f + 1, lanes] = value
             values.append(value)
         density, vel_x, vel_y, vel_z, pressure = values
-        cos_p = point_ref[0:1, lanes]
-        sin_p = point_ref[1:2, lanes]
-        weight = point_ref[3:4, lanes] * norm_scale
+        cos_p, sin_p = sincos(point_ref[0:1, lanes])
+        weight = point_ref[2:3, lanes] * norm_scale
         flux = weight * density * (vel_x * cos_p + vel_y * sin_p)
         push = weight * pressure
         for at, row in enumerate(
             (
                 cos_p,
                 sin_p,
-                point_ref[2:3, lanes],
+                point_ref[1:2, lanes],
                 flux,
                 push * cos_p + flux * vel_x,
                 push * sin_p + flux * vel_y,
@@ -207,9 +333,23 @@
             terms = [a + b for a, b in zip(terms[0::2], terms[1::2])]
         return terms[0]
 
-    def observers(g, carry):
-        at = pl.ds(pl.multiple_of(g * 8, 8), 8)
-        obs_x, obs_y, obs_z = obs_x_ref[at, :], obs_y_ref[at, :], obs_z_ref[at, :]
+    count = obs_ref.shape[1]
+    groups, own = count // 8, stage.shape[1]
+    per_group = 8 // own
+    met(devices)
+
+    def observers(step, carry):
+        g = lax.rem(me // per_group + 1 + step, groups)
+        column_of = lax.broadcasted_iota(jnp.int32, (8, count), 0) + g * 8
+        chosen = slot_ref[...] == column_of
+        spread = [
+            jnp.broadcast_to(
+                jnp.sum(jnp.where(chosen, obs_ref[i : i + 1, :], 0.0), axis=1, keepdims=True),
+                (8, 128),
+            )
+            for i in range(4)
+        ]
+        obs_x, obs_y, obs_z, radius = spread
         for part in range(points // tile):
             state = []
             for u in range(group):
@@ -258,10 +398,21 @@
         result = jnp.zeros((8, 128), F32)
         for column in range(8 * BASIS + 1):
             result = jnp.where(lane == column, jnp.sum(acc[column], axis=1, keepdims=True), result)
-        sums_ref[at, :] = result
+        result = result * radius
+        for j in range(per_group):
+            other = g * per_group + j
+            stage[other] = result[j * own : (j + 1) * own, :]
+
+            @pl.when(other != me)
+            def _():
+                transfer(stage, landing, send_sems, recv_sems, other, me).start()
+
         return carry
 
-    lax.fori_loop(0, obs_x_ref.shape[0] // 8, observers, 0)
+    lax.fori_loop(0, groups, observers, 0)
+    landing[me] = stage[me]
+    finish(devices, stage, landing, send_sems, recv_sems)
+    sums_ref[...] = jnp.sum(landing[...], axis=0)
 
 
 def expansion():
@@ -315,58 +466,70 @@
     norm_scale = 1.0 / math.sqrt(points * devices)
     target = owner.reshape(1, points)
 
-    send, rank = pl.pallas_call(
+    own = observers // devices
+    vmem = pl.BlockSpec(memory_space=pltpu.VMEM)
+    sems = [pltpu.SemaphoreType.DMA((devices,)), pltpu.SemaphoreType.DMA((devices,))]
+
+    def params(number):
+        return pltpu.CompilerParams(collective_id=number, has_side_effects=True)
+
+    recv, ids, rank = pl.pallas_call(
         functools.partial(pack_kernel, devices, cap),
         out_shape=(
             jax.ShapeDtypeStruct((devices, 4, cap), F32),
+            jax.ShapeDtypeStruct((devices, cap), jnp.int32),
             jax.ShapeDtypeStruct((1, points), jnp.int32),
         ),
+        scratch_shapes=[pltpu.VMEM((devices, 4, cap), F32), pltpu.VMEM((devices, 4, cap), F32)] + sems,
+        compiler_params=params(0),
         name="pack",
     )(target, local_element.reshape(1, points), ref_coords)
-    recv = lax.all_to_all(send, AXES, split_axis=0, concat_axis=0, tiled=True)
-    ids = recv[:, 0, :].reshape(devices * cap).astype(jnp.int32)
-    vmem = pl.BlockSpec(memory_space=pltpu.VMEM)
-    served = pl.pallas_call(
+    half_shape = (max(1, cap // 128), min(cap, 128), 512)
+    replies = pl.pallas_call(
         interp_kernel,
         out_shape=jax.ShapeDtypeStruct((devices, FIELDS, cap), F32),
         in_specs=[pl.BlockSpec(memory_space=pltpu.SMEM), vmem, vmem, vmem],
         out_specs=vmem,
         scratch_shapes=[
             pltpu.VMEM((element_fields.shape[0], 8, 512), F32),
-            pltpu.VMEM((max(1, cap // 128), min(cap, 128), 512), F32),
-        ],
+            pltpu.VMEM(half_shape, F32),
+            pltpu.VMEM(half_shape, F32),
+            pltpu.VMEM((devices, FIELDS, cap), F32),
+            pltpu.VMEM((devices, FIELDS, cap), F32),
+        ]
+        + sems,
+        compiler_params=params(1),
         name="interp",
-    )(ids, recv, jnp.asarray(expansion(), BF16), element_fields)
-    replies = lax.all_to_all(served, AXES, split_axis=0, concat_axis=0, tiled=True)
-
-    chosen = observer_slot[:, None] == jnp.arange(observers, dtype=jnp.int32)[None, :]
-    in_order = lambda x: jnp.sum(jnp.where(chosen, x[:, None], 0.0), axis=0)
-    radius = in_order(obs_radius)
-    obs_x = in_order(obs_radius * jnp.cos(obs_angle))
-    obs_y = in_order(obs_radius * jnp.sin(obs_angle))
-    obs_z = in_order(obs_axial)
-    spread = lambda x: jnp.broadcast_to(x[:, None], (observers, 128))
-    point_rows = jnp.stack([jnp.cos(point_angle), jnp.sin(point_angle), point_axial, panel_weight])
-    surface_values, sums = pl.pallas_call(
+    )(ids, recv, jnp.asarray(expansion(), BF16), element_fields.transpose(1, 0, 2))
+
+    obs_rows = jnp.stack(
+        [obs_radius * jnp.cos(obs_angle), obs_radius * jnp.sin(obs_angle), obs_axial, obs_radius]
+    )
+    surface_values, summed = pl.pallas_call(
         functools.partial(spectra_kernel, norm_scale),
         out_shape=(
             jax.ShapeDtypeStruct((FIELDS, points), F32),
-            jax.ShapeDtypeStruct((observers, 128), F32),
+            jax.ShapeDtypeStruct((own, 128), F32),
         ),
         scratch_shapes=[
             pltpu.VMEM((7, 8, points), F32),
             pltpu.VMEM((8 * BASIS + 1, 8, 128), F32),
-        ],
+            pltpu.VMEM((devices, own, 128), F32),
+            pltpu.VMEM((devices, own, 128), F32),
+        ]
+        + sems,
+        compiler_params=params(2),
         name="spectra",
-    )(replies, target, rank, point_rows, spread(obs_x), spread(obs_y), spread(obs_z))
-
-    own = observers // devices
-    gathered = lax.all_to_all(sums, AXES, split_axis=0, concat_axis=0, tiled=True)
-    summed = jnp.sum(gathered.reshape(devices, own, 128), axis=0)
-    me = lax.axis_index(AXES)
-    own_radius = lax.dynamic_slice(radius, (me * own,), (own,))
+    )(
+        replies,
+        target,
+        rank,
+        jnp.stack([point_angle, point_axial, panel_weight]),
+        obs_rows,
+        observer_slot.reshape(1, observers),
+    )
     recombined = jnp.dot(
-        summed * own_radius[:, None], jnp.asarray(recombination()), precision=lax.Precision.HIGHEST
+        summed, jnp.asarray(recombination()), precision=lax.Precision.HIGHEST
     )
     cos_sum, sin_sum = recombined[:, :harmonics].T, recombined[:, harmonics:].T
     cos_f, sin_f = jnp.cos(step_phase)[:, None], jnp.sin(step_phase)[:, None]

time: 108 us -> 82.7 us (0.77)
  waiting for transfers between devices: 19 us -> 0 us
  Pallas kernels: 62.2 us -> 77.2 us
  starting transfers between devices: 14.1 us -> 0 us
  local copies, waits for them, and re-layouts: 7.83 us -> 1.57 us
    all_to_all x3 -> x0, waiting for transfers between devices: 19 us -> none  [the longest x1 9.06 us: on_device(): lax.all_to_all(served, AXES, split_axis=0, concat_axis=0, tiled=True)]
    all_to_all x3 -> x0, starting transfers between devices: 14.1 us -> none  [the longest x1 7.33 us: on_device(): recv = lax.all_to_all(send, AXES, split_axis=0, concat_axis=0, tiled=True)]
    pallas_call x1, Pallas kernels: 5.84 us -> 15.4 us  [on_device(): pl.pallas_call(functools.partial(pack_kernel, devices, cap), out_shape=(j...]
    pallas_call x1, Pallas kernels: 24.8 us -> 32.3 us  [on_device(): pl.pallas_call(functools.partial(spectra_kernel, norm_scale), out_shape=(...]
    unnamed x23 -> x19, local copies, waits for them, and re-layouts: 5.44 us -> 1.51 us
    broadcast_in_dim x3 -> x0, local copies, waits for them, and re-layouts: 2.23 us -> none  [on_device(): spread = lambda x: jnp.broadcast_to(x[:, None], (observers, 128))]
    pallas_call x1, Pallas kernels: 31.5 us -> 29.4 us  [on_device(): pl.pallas_call(interp_kernel, out_shape=jax.ShapeDtypeStruct((devices, FI...]
  transfers between devices with their start and end apart: 3 -> 0, of which waited for: 3 -> 0; matrix products, arithmetic and copies ran while one was open for 7% -> 0% of each run, Pallas kernels for 0% -> 0%
where the time goes in v2:
time: 82.7 us; the launch traced here: 82.3 us
  Pallas kernels  77.2 us (93%)
  other arithmetic  1.97 us (2%)
  local copies, waits for them, and re-layouts  1.57 us (2%)
  matrix products  0.83 us (1%)
    pallas_call x1, Pallas kernels, on_device(): pl.pallas_call(functools.partial(spectra_kernel, norm_scale), out_shape=(...  32.3 us
    pallas_call x1, Pallas kernels, on_device(): pl.pallas_call(interp_kernel, out_shape=jax.ShapeDtypeStruct((devices, FI...  29.4 us
    pallas_call x1, Pallas kernels, on_device(): pl.pallas_call(functools.partial(pack_kernel, devices, cap), out_shape=(j...  15.4 us

profile of v2, /device:TPU:0, one launch (start us, length us, event | category | flops | bytes accessed | tf_op | source)
XLA Modules:
  0.0 82.3 jit_solution(8322450537354805567)
XLA Ops:
  0.6 0.0 copy-start
  0.6 0.0 copy-start.5
  0.7 0.0 copy-start.6
  0.7 0.0 copy-start.7
  0.7 0.0 copy-start.3
  0.7 0.0 copy-start.2
  0.7 0.0 copy-start.1
  0.7 0.0 copy-start.8
  0.7 0.0 copy-start.4
  0.7 15.4 %pack.1 = (f32[32,4,256]{2,1,0:T(4,128)}, s32[32,256]{1,0:T(8,128)}, s32[1,2048]{1,0:T(1,128)}) custom-call(s32[1,2048]{1,0:T(1,128)} %bitcast.22, s32[1,2048]{1,0:T(1,128)} %bitcast.27, f32[3,2048]{1,0:T(4,128)} %coords_ref.1), custom_call_target="tpu_custom_call" | custom-call | tf_op jit(solution)/shard_map/pack/pallas_call | solution.py:476
  16.2 29.4 %interp.1.replies_ref = f32[32,5,256]{2,1,0:T(8,128)} custom-call(s32[32,256]{1,0:T(8,128)} %get-tuple-element.7.ids_ref, f32[32,4,256]{2,1,0:T(4,128)} %get-tuple-element.8.recv_ref, bf16[72,768]{1,0:T(8,128)(2,1)} %constant.4.clone.expand_ref, bf16[5,512,512]{2,1,0:T(8,128)(2,1)} %bitcast.21), custom_call_target="tpu_custom_call" | custom-call | tf_op jit(solution)/shard_map/interp/pallas_call | solution.py:488
  45.6 0.0 copy-done.5
  45.6 0.0 copy-done.6
  45.7 0.0 copy-done.7
  45.7 0.6 pad_maximum_fusion.1.obs_ref
  46.3 0.0 copy-done.3
  46.3 0.0 copy-done.2
  46.3 0.0 copy-done.1
  46.3 0.6 pad_maximum_fusion.point_ref
  46.9 32.3 %spectra.1 = (f32[5,2048]{1,0:T(8,128)}, f32[8,128]{1,0:T(8,128)}) custom-call(f32[32,5,256]{2,1,0:T(8,128)} %interp.1.replies_ref, s32[1,2048]{1,0:T(1,128)} %bitcast.23, s32[1,2048]{1,0:T(1,128)} %get-tuple-element.9.rank_ref, f32[3,2048]{1,0:T(4,128)} %pad_maximum_fusion.point_ref, f32[4,256]{1,0:T(4,128)} %pad_maximum_fusion.1.obs_ref, s32[1,256]{1,0:T(1,128)} %bitcast.31), custom_call_target="tpu_custom_call" | custom-call | tf_op jit(solution)/shard_map/spectra/pallas_call | solution.py:508
  79.3 0.0 copy-done
  79.3 0.8 %fusion.1 = f32[8,64]{1,0:T(8,128)S(1)} fusion(f32[8,128]{1,0:T(8,128)} %get-tuple-element.11, f32[128,64]{1,0:T(8,128)S(1)} %copy-done), kind=kOutput, calls=%fused_computation.8 | convolution fusion | flops 786432 | bytes 38912 | tf_op jit(solution)/shard_map/dot_general | solution.py:531
  80.1 0.0 copy-done.8
  80.1 0.1 fusion
  80.2 0.1 subtract_bitcast_fusion
  80.2 0.0 copy-done.4
  80.2 0.6 maximum_add_fusion
  80.8 1.5 %copy.18 = f32[5,2048]{1,0:T(8,128)} copy(f32[5,2048]{1,0:T(8,128)} %get-tuple-element.20) | data formatting | bytes 81920
  (1 shorter events, 0.0 us)
Async XLA Ops:
  0.6 78.6 %copy-start = (f32[128,64]{1,0:T(8,128)S(1)}, f32[128,64]{1,0:T(8,128)}, u32[]{:S(2)}) copy-start(f32[128,64]{1,0:T(8,128)} %constant.5.clone) | copy-start | bytes 98308
  0.6 45.0 %copy-start.5 = (f32[256]{0:T(256)S(1)}, f32[256]{0:T(256)}, u32[]{:S(2)}) copy-start(f32[256]{0:T(256)} %param.22) | copy-start | bytes 3076
  0.7 45.0 %copy-start.6 = (f32[256]{0:T(256)S(1)}, f32[256]{0:T(256)}, u32[]{:S(2)}) copy-start(f32[256]{0:T(256)} %param.23) | copy-start | bytes 3076
  0.7 45.0 %copy-start.7 = (f32[256]{0:T(256)S(1)}, f32[256]{0:T(256)}, u32[]{:S(2)}) copy-start(f32[256]{0:T(256)} %param.24) | copy-start | bytes 3076
  0.7 45.6 %copy-start.3 = (f32[2048]{0:T(1024)S(1)}, f32[2048]{0:T(1024)}, u32[]{:S(2)}) copy-start(f32[2048]{0:T(1024)} %param.19) | copy-start | bytes 24580
  0.7 45.6 %copy-start.2 = (f32[2048]{0:T(1024)S(1)}, f32[2048]{0:T(1024)}, u32[]{:S(2)}) copy-start(f32[2048]{0:T(1024)} %param.20) | copy-start | bytes 24580
  0.7 45.6 %copy-start.1 = (f32[2048]{0:T(1024)S(1)}, f32[2048]{0:T(1024)}, u32[]{:S(2)}) copy-start(f32[2048]{0:T(1024)} %param.21) | copy-start | bytes 24580
  0.7 79.4 %copy-start.8 = (f32[32]{0:T(128)S(1)}, f32[32]{0:T(128)}, u32[]{:S(2)}) copy-start(f32[32]{0:T(128)} %param.25) | copy-start | bytes 388
  0.7 79.5 %copy-start.4 = (f32[2,32,8]{1,2,0:T(8,128)S(1)}, f32[2,32,8]{1,2,0:T(8,128)}, u32[]{:S(2)}) copy-start(f32[2,32,8]{1,2,0:T(8,128)} %param.27) | copy-start | bytes 6148

commit v3 on v2

--- a/solution.py
+++ b/solution.py
@@ -268,6 +268,24 @@
     return first, second
 
 
+def sincos_by_doubling(angle):
+    x = angle * 0.125
+    z = x * x
+    sine = 1.0 / 362880.0 * z - 1.0 / 5040.0
+    sine = sine * z + 1.0 / 120.0
+    sine = sine * z - 1.0 / 6.0
+    sine = (sine * z + 1.0) * x
+    cosine = -1.0 / 3628800.0 * z + 1.0 / 40320.0
+    cosine = cosine * z - 1.0 / 720.0
+    cosine = cosine * z + 1.0 / 24.0
+    cosine = cosine * z - 0.5
+    cosine = cosine * z + 1.0
+    for _ in range(3):
+        twice = sine + sine
+        cosine, sine = 1.0 - twice * sine, twice * cosine
+    return cosine, sine
+
+
 def spectra_kernel(
     norm_scale,
     replies_ref,
@@ -280,6 +298,7 @@
     sums_ref,
     rows,
     acc,
+    observer,
     stage,
     landing,
     send_sems,
@@ -336,20 +355,16 @@
     count = obs_ref.shape[1]
     groups, own = count // 8, stage.shape[1]
     per_group = 8 // own
+    chosen = slot_ref[...] == lax.broadcasted_iota(jnp.int32, (count, count), 0)
+    for i in range(4):
+        column = jnp.sum(jnp.where(chosen, obs_ref[i : i + 1, :], 0.0), axis=1, keepdims=True)
+        observer[i] = jnp.broadcast_to(column, (count, 128))
     met(devices)
 
     def observers(step, carry):
         g = lax.rem(me // per_group + 1 + step, groups)
-        column_of = lax.broadcasted_iota(jnp.int32, (8, count), 0) + g * 8
-        chosen = slot_ref[...] == column_of
-        spread = [
-            jnp.broadcast_to(
-                jnp.sum(jnp.where(chosen, obs_ref[i : i + 1, :], 0.0), axis=1, keepdims=True),
-                (8, 128),
-            )
-            for i in range(4)
-        ]
-        obs_x, obs_y, obs_z, radius = spread
+        at = pl.ds(pl.multiple_of(g * 8, 8), 8)
+        obs_x, obs_y, obs_z = observer[0, at, :], observer[1, at, :], observer[2, at, :]
         for part in range(points // tile):
             state = []
             for u in range(group):
@@ -362,14 +377,17 @@
                 rough = square * inverse
                 half = 0.5 * inverse
                 dist = rough + half * (square - rough * rough)
-                inverse = inverse + inverse * (0.5 - half * (square * inverse))
                 along = dx * rows[4, :, lanes] + dy * rows[5, :, lanes] + dz * rows[6, :, lanes]
                 amp = inverse * (rows[3, :, lanes] + inverse * along)
-                c1, s1 = sincos(dist * omega_base)
-                c2, s2 = c1 * c1 - s1 * s1, 2.0 * c1 * s1
-                c4, s4 = c2 * c2 - s2 * s2, 2.0 * c2 * s2
-                c8, s8 = c4 * c4 - s4 * s4, 2.0 * c4 * s4
-                c16, s16 = c8 * c8 - s8 * s8, 2.0 * c8 * s8
+                c1, s1 = sincos_by_doubling(dist * omega_base)
+                t1 = s1 + s1
+                c2, s2 = 1.0 - t1 * s1, t1 * c1
+                t2 = s2 + s2
+                c4, s4 = 1.0 - t2 * s2, t2 * c2
+                t4 = s4 + s4
+                c8, s8 = 1.0 - t4 * s4, t4 * c4
+                t8 = s8 + s8
+                c16, s16 = 1.0 - t8 * s8, t8 * c8
                 c24 = c16 * c8 - s16 * s8
                 state.append(
                     [amp, jnp.zeros_like(amp), amp * c1, amp * s1, 2.0 * c1, 2.0 * c8, 2.0 * c16, 2.0 * c24]
@@ -398,7 +416,7 @@
         result = jnp.zeros((8, 128), F32)
         for column in range(8 * BASIS + 1):
             result = jnp.where(lane == column, jnp.sum(acc[column], axis=1, keepdims=True), result)
-        result = result * radius
+        result = result * observer[3, at, :]
         for j in range(per_group):
             other = g * per_group + j
             stage[other] = result[j * own : (j + 1) * own, :]
@@ -514,6 +532,7 @@
         scratch_shapes=[
             pltpu.VMEM((7, 8, points), F32),
             pltpu.VMEM((8 * BASIS + 1, 8, 128), F32),
+            pltpu.VMEM((4, observers, 128), F32),
             pltpu.VMEM((devices, own, 128), F32),
             pltpu.VMEM((devices, own, 128), F32),
         ]

time: 82.7 us -> 78.4 us (0.948)
  Pallas kernels: 77.2 us -> 73 us
    pallas_call x1, Pallas kernels: 32.3 us -> 28.1 us  [on_device(): pl.pallas_call(functools.partial(spectra_kernel, norm_scale), out_shape=(...]
where the time goes in v3:
time: 78.4 us; the launch traced here: 78.1 us
  Pallas kernels  73 us (93%)
  other arithmetic  1.97 us (3%)
  local copies, waits for them, and re-layouts  1.57 us (2%)
  matrix products  0.83 us (1%)
    pallas_call x1, Pallas kernels, on_device(): pl.pallas_call(interp_kernel, out_shape=jax.ShapeDtypeStruct((devices, FI...  29.4 us
    pallas_call x1, Pallas kernels, on_device(): pl.pallas_call(functools.partial(spectra_kernel, norm_scale), out_shape=(...  28.1 us
    pallas_call x1, Pallas kernels, on_device(): pl.pallas_call(functools.partial(pack_kernel, devices, cap), out_shape=(j...  15.4 us

profile of v3, /device:TPU:0, one launch (start us, length us, event | category | flops | bytes accessed | tf_op | source)
XLA Modules:
  0.0 78.1 jit_solution(6746946793723764991)
XLA Ops:
  0.6 0.0 copy-start
  0.6 0.0 copy-start.5
  0.7 0.0 copy-start.6
  0.7 0.0 copy-start.7
  0.7 0.0 copy-start.3
  0.7 0.0 copy-start.2
  0.7 0.0 copy-start.1
  0.7 0.0 copy-start.8
  0.7 0.0 copy-start.4
  0.7 15.4 %pack.1 = (f32[32,4,256]{2,1,0:T(4,128)}, s32[32,256]{1,0:T(8,128)}, s32[1,2048]{1,0:T(1,128)}) custom-call(s32[1,2048]{1,0:T(1,128)} %bitcast.22, s32[1,2048]{1,0:T(1,128)} %bitcast.27, f32[3,2048]{1,0:T(4,128)} %coords_ref.1), custom_call_target="tpu_custom_call" | custom-call | tf_op jit(solution)/shard_map/pack/pallas_call | solution.py:494
  16.2 29.4 %interp.1.replies_ref = f32[32,5,256]{2,1,0:T(8,128)} custom-call(s32[32,256]{1,0:T(8,128)} %get-tuple-element.7.ids_ref, f32[32,4,256]{2,1,0:T(4,128)} %get-tuple-element.8.recv_ref, bf16[72,768]{1,0:T(8,128)(2,1)} %constant.4.clone.expand_ref, bf16[5,512,512]{2,1,0:T(8,128)(2,1)} %bitcast.21), custom_call_target="tpu_custom_call" | custom-call | tf_op jit(solution)/shard_map/interp/pallas_call | solution.py:506
  45.6 0.0 copy-done.5
  45.6 0.0 copy-done.6
  45.7 0.0 copy-done.7
  45.7 0.6 pad_maximum_fusion.1.obs_ref
  46.3 0.0 copy-done.3
  46.3 0.0 copy-done.2
  46.3 0.0 copy-done.1
  46.3 0.6 pad_maximum_fusion.point_ref
  46.9 28.1 %spectra.1 = (f32[5,2048]{1,0:T(8,128)}, f32[8,128]{1,0:T(8,128)}) custom-call(f32[32,5,256]{2,1,0:T(8,128)} %interp.1.replies_ref, s32[1,2048]{1,0:T(1,128)} %bitcast.23, s32[1,2048]{1,0:T(1,128)} %get-tuple-element.9.rank_ref, f32[3,2048]{1,0:T(4,128)} %pad_maximum_fusion.point_ref, f32[4,256]{1,0:T(4,128)} %pad_maximum_fusion.1.obs_ref, s32[1,256]{1,0:T(1,128)} %bitcast.31), custom_call_target="tpu_custom_call" | custom-call | tf_op jit(solution)/shard_map/spectra/pallas_call | solution.py:526
  75.0 0.0 copy-done
  75.0 0.8 %fusion.1 = f32[8,64]{1,0:T(8,128)S(1)} fusion(f32[8,128]{1,0:T(8,128)} %get-tuple-element.11, f32[128,64]{1,0:T(8,128)S(1)} %copy-done), kind=kOutput, calls=%fused_computation.8 | convolution fusion | flops 786432 | bytes 38912 | tf_op jit(solution)/shard_map/dot_general | solution.py:550
  75.9 0.0 copy-done.8
  75.9 0.1 fusion
  75.9 0.1 subtract_bitcast_fusion
  76.0 0.0 copy-done.4
  76.0 0.6 maximum_add_fusion
  76.6 1.5 %copy.18 = f32[5,2048]{1,0:T(8,128)} copy(f32[5,2048]{1,0:T(8,128)} %get-tuple-element.20) | data formatting | bytes 81920
  (1 shorter events, 0.0 us)
Async XLA Ops:
  0.6 74.4 %copy-start = (f32[128,64]{1,0:T(8,128)S(1)}, f32[128,64]{1,0:T(8,128)}, u32[]{:S(2)}) copy-start(f32[128,64]{1,0:T(8,128)} %constant.5.clone) | copy-start | bytes 98308
  0.6 45.0 %copy-start.5 = (f32[256]{0:T(256)S(1)}, f32[256]{0:T(256)}, u32[]{:S(2)}) copy-start(f32[256]{0:T(256)} %param.22) | copy-start | bytes 3076
  0.7 45.0 %copy-start.6 = (f32[256]{0:T(256)S(1)}, f32[256]{0:T(256)}, u32[]{:S(2)}) copy-start(f32[256]{0:T(256)} %param.23) | copy-start | bytes 3076
  0.7 45.0 %copy-start.7 = (f32[256]{0:T(256)S(1)}, f32[256]{0:T(256)}, u32[]{:S(2)}) copy-start(f32[256]{0:T(256)} %param.24) | copy-start | bytes 3076
  0.7 45.6 %copy-start.3 = (f32[2048]{0:T(1024)S(1)}, f32[2048]{0:T(1024)}, u32[]{:S(2)}) copy-start(f32[2048]{0:T(1024)} %param.19) | copy-start | bytes 24580
  0.7 45.6 %copy-start.2 = (f32[2048]{0:T(1024)S(1)}, f32[2048]{0:T(1024)}, u32[]{:S(2)}) copy-start(f32[2048]{0:T(1024)} %param.20) | copy-start | bytes 24580
  0.7 45.6 %copy-start.1 = (f32[2048]{0:T(1024)S(1)}, f32[2048]{0:T(1024)}, u32[]{:S(2)}) copy-start(f32[2048]{0:T(1024)} %param.21) | copy-start | bytes 24580
  0.7 75.2 %copy-start.8 = (f32[32]{0:T(128)S(1)}, f32[32]{0:T(128)}, u32[]{:S(2)}) copy-start(f32[32]{0:T(128)} %param.25) | copy-start | bytes 388
  0.7 75.3 %copy-start.4 = (f32[2,32,8]{1,2,0:T(8,128)S(1)}, f32[2,32,8]{1,2,0:T(8,128)}, u32[]{:S(2)}) copy-start(f32[2,32,8]{1,2,0:T(8,128)} %param.27) | copy-start | bytes 6148
